TPU v7x, 256 devices: a whole 4x4x8 slice. The times are simulated.
256 devices in a mesh: lat: 8 (over z_lo, core), lon: 8 (over z_hi, x), chan: 4 (over y).
Axes of the slice: x: 4, y: 4, z: 8 (z_hi: 2, z_lo: 4; z = z_hi * 4 + z_lo), core: 2. Of those that a mesh axis runs over, the one named last changes fastest.
Arguments:
- queries: bfloat16 [128, 64, 2560], P('lat', 'lon', 'chan'), may hold values from -8 to 8
- keys: bfloat16 [128, 64, 2560], P('lat', 'lon', 'chan'), may hold values from -8 to 8
- values: bfloat16 [128, 64, 2560], P('lat', 'lon', 'chan'), may hold values from -6 to 6
- attn_out: bfloat16 [128, 64, 2560], P('lat', 'lon', 'chan'), may hold values from -6 to 6
- grad_out: bfloat16 [128, 64, 5120], P('lat', 'lon', 'chan'), may hold values from -6 to 6
- w_out: bfloat16 [5120, 2560], P(('lat', 'lon'), 'chan'), may hold values from -0.078125 to 0.078125
- bias_table: float32 [20, 25, 13], P('chan'), may hold values from -5 to 5
- key_mask: int32 [128, 64], replicated, may hold values 0 or 1
Outputs:
- grad_queries: bfloat16 [128, 64, 2560], P('lat', 'lon', 'chan')
- grad_keys: bfloat16 [128, 64, 2560], P('lat', 'lon', 'chan')
- grad_values: bfloat16 [128, 64, 2560], P('lat', 'lon', 'chan')
- grad_wout: float32 [5120, 2560], P(('lat', 'lon'), 'chan')
- grad_table: float32 [20, 25, 13], P('chan')
All inputs are finite; a program needn't handle non-finite values.
Results may differ from a plain program's by a relative error of at most 0.007.
Values may be sent and summed in bfloat16 or wider, within the bound.
No kernel may reach another device: no remote copies, remote signals or barrier semaphores. Data moves between devices by JAX's collectives and lax.ppermute only.
A program may use at most 128 MiB of HBM per device.

v0:
```python
import jax
import jax.numpy as jnp
from jax import lax
from jax.sharding import PartitionSpec as P

HEAD_DIM = 128
WIN = 13


def extended_2(value, sides, width, wrap):
    for axis, dim in sides:
        count, length = (lax.axis_size(axis), value.shape[dim])
        up = [(i, (i + 1) % count) for i in range(count if wrap else count - 1)]
        down = [(j, i) for i, j in up]
        last = lax.slice_in_dim(value, length - width, length, axis=dim)
        leading = lax.slice_in_dim(value, 0, width, axis=dim)
        before = lax.ppermute(last, axis, up)
        after = lax.ppermute(leading, axis, down)
        value = jnp.concatenate([before, value, after], axis=dim)
    return value


def fold_lon(extended, core_width):
    full_width = extended.shape[2]
    reach_cells = (full_width - core_width) // 2
    rim_cells = jnp.concatenate(
        [extended[:, :, :reach_cells], extended[:, :, full_width - reach_cells :]], axis=2
    )
    received = extended_2(rim_cells.astype(jnp.bfloat16), (("lon", 2),), reach_cells, True).astype(
        rim_cells.dtype
    )
    middle = extended[:, :, reach_cells : full_width - reach_cells]
    front_add = jnp.pad(
        received[:, :, :reach_cells], ((0, 0), (0, 0), (0, core_width - reach_cells), (0, 0))
    )
    back_add = jnp.pad(
        received[:, :, 3 * reach_cells :], ((0, 0), (0, 0), (core_width - reach_cells, 0), (0, 0))
    )
    return middle + front_add + back_add


def fold_lat(extended, core_width):
    full_width = extended.shape[1]
    reach_cells = (full_width - core_width) // 2
    rim_cells = jnp.concatenate(
        [extended[:, :reach_cells], extended[:, full_width - reach_cells :]], axis=1
    )
    received = extended_2(rim_cells.astype(jnp.bfloat16), (("lat", 1),), reach_cells, False).astype(
        rim_cells.dtype
    )
    middle = extended[:, reach_cells : full_width - reach_cells]
    front_add = jnp.pad(
        received[:, :reach_cells], ((0, 0), (0, core_width - reach_cells), (0, 0), (0, 0))
    )
    back_add = jnp.pad(
        received[:, 3 * reach_cells :], ((0, 0), (core_width - reach_cells, 0), (0, 0), (0, 0))
    )
    return middle + front_add + back_add


def local(queries, keys, values, attn_out, grad_out, w_out, bias_table, key_mask):
    lat_rows, lon_cols, chan_width = queries.shape
    head_count = bias_table.shape[0]
    reach_cells = WIN // 2
    score_scale = HEAD_DIM ** (-0.5)
    tokens = lat_rows * lon_cols
    ext_rows = lat_rows + 2 * reach_cells
    ext_cols = lon_cols + 2 * reach_cells
    row_block = 4
    key_span = row_block + WIN - 1
    block_count = lat_rows // row_block
    block_rows = row_block * lon_cols
    block_keys = key_span * ext_cols
    offset_rows = 2 * WIN - 1
    low_pad = row_block - 1
    lat_total = lat_rows * lax.axis_size("lat")
    lon_total = lon_cols * lax.axis_size("lon")
    contract_lead = (((0,), (0,)), ((), ()))
    full_grad = lax.all_gather(grad_out, "chan", axis=2, tiled=True).reshape(tokens, -1)
    grad_cols = jnp.transpose(full_grad)
    slab_part = grad_cols
    grad_attn = lax.dot_general(
        slab_part,
        lax.all_gather(w_out, ("lat", "lon"), axis=0, tiled=True),
        contract_lead,
        preferred_element_type=jnp.float32,
    ).astype(jnp.bfloat16)
    kv_pair = jnp.stack([keys, values])
    extended = extended_2(kv_pair, (("lat", 1), ("lon", 2)), reach_cells, True)
    lat_first = lax.axis_index("lat") * lat_rows
    lon_first = lax.axis_index("lon") * lon_cols
    ext_col = lon_first - reach_cells + jnp.arange(ext_cols, dtype=jnp.int32)
    wrap_col = ext_col % lon_total
    mask_cols = jnp.take(key_mask, wrap_col, axis=1)
    mark_cols = wrap_col % 4 == 0
    rel_lon = (
        jnp.arange(ext_cols, dtype=jnp.int32)[None, :]
        - jnp.arange(lon_cols, dtype=jnp.int32)[:, None]
    )
    in_lon = (rel_lon >= 0) & (rel_lon < WIN)
    lon_pick = jnp.clip(rel_lon, 0, WIN - 1)
    lon_table = jnp.take(bias_table, lon_pick, axis=2).transpose(0, 2, 1, 3)
    table_pad = jnp.pad(lon_table, ((0, 0), (0, 0), (low_pad, low_pad), (0, 0)))
    query_heads = queries.reshape(lat_rows, lon_cols, head_count, HEAD_DIM)
    grad_heads = grad_attn.reshape(lat_rows, lon_cols, head_count, HEAD_DIM)

    def block_step(state_pair, block_index):
        grad_pair, table_acc = state_pair
        local_first = block_index * row_block
        top_row = lat_first + local_first
        key_first = jnp.clip(top_row - reach_cells, 0, lat_total - key_span)
        key_local = key_first - (lat_first - reach_cells)
        query_rows = top_row + jnp.arange(row_block, dtype=jnp.int32)
        window_first = jnp.clip(query_rows - reach_cells, 0, lat_total - WIN)
        key_glob = key_first + jnp.arange(key_span, dtype=jnp.int32)
        in_lat = (key_glob[None, :] >= window_first[:, None]) & (
            key_glob[None, :] < window_first[:, None] + WIN
        )
        mask_rows = lax.dynamic_slice_in_dim(mask_cols, key_first, key_span, 0)
        valid_keys = (mask_rows == 1) | (key_glob % 4 == 0)[:, None] & mark_cols[None, :]
        allowed = in_lat[:, None, :, None] & in_lon[None, :, None, :] & valid_keys[None, None, :, :]
        allowed = allowed.reshape(block_rows, block_keys)
        shifts = key_first - query_rows + (WIN - 1) + low_pad
        bias_parts = [
            lax.dynamic_slice_in_dim(table_pad, shifts[row_pos], key_span, 2)
            for row_pos in range(row_block)
        ]
        bias_rows = jnp.stack(bias_parts, axis=1).reshape(head_count, block_rows, block_keys)
        query_block = lax.dynamic_slice_in_dim(query_heads, local_first, row_block, 0).reshape(
            block_rows, head_count, HEAD_DIM
        )
        grad_block = lax.dynamic_slice_in_dim(grad_heads, local_first, row_block, 0).reshape(
            block_rows, head_count, HEAD_DIM
        )
        pair_block = lax.dynamic_slice_in_dim(extended, key_local, key_span, 1).reshape(
            2, block_keys, head_count, HEAD_DIM
        )
        key_block = pair_block[0]
        value_block = pair_block[1]
        scores = (
            score_scale
            * jnp.einsum("qhd,khd->hqk", query_block, key_block, preferred_element_type=jnp.float32)
            + bias_rows
        )
        scores = jnp.where(allowed[None], scores, -1e30)
        row_max = jnp.max(scores, axis=2, keepdims=True)
        weights_exp = jnp.exp(scores - row_max)
        prob_rows = weights_exp / jnp.sum(weights_exp, axis=2, keepdims=True)
        grad_prob = jnp.einsum(
            "qhd,khd->hqk", grad_block, value_block, preferred_element_type=jnp.float32
        )
        row_delta = jnp.sum(prob_rows * grad_prob, axis=2, keepdims=True)
        dscore = prob_rows * (grad_prob - row_delta)
        score_grid = dscore.reshape(head_count, row_block, lon_cols, key_span, ext_cols)
        score_grid = score_grid.transpose(0, 1, 3, 2, 4).reshape(
            head_count, row_block, key_span, lon_cols * ext_cols
        )
        for row_pos in range(row_block):
            prior_sum = lax.dynamic_slice_in_dim(table_acc, shifts[row_pos], key_span, 1)
            table_acc = lax.dynamic_update_slice_in_dim(
                table_acc, prior_sum + score_grid[:, row_pos], shifts[row_pos], 1
            )
        dscore_low = dscore.astype(jnp.bfloat16)
        prob_low = prob_rows.astype(jnp.bfloat16)
        grad_query = (
            score_scale
            * jnp.einsum("hqk,khd->qhd", dscore_low, key_block, preferred_element_type=jnp.float32)
        ).astype(jnp.bfloat16)
        key_part = score_scale * jnp.einsum(
            "hqk,qhd->khd", dscore_low, query_block, preferred_element_type=jnp.float32
        )
        value_part = jnp.einsum(
            "hqk,qhd->khd", prob_low, grad_block, preferred_element_type=jnp.float32
        )
        new_part = jnp.stack([key_part, value_part]).reshape(2, key_span, ext_cols, chan_width)
        prior_pair = lax.dynamic_slice_in_dim(grad_pair, key_local, key_span, 1)
        grad_pair = lax.dynamic_update_slice_in_dim(grad_pair, prior_pair + new_part, key_local, 1)
        return ((grad_pair, table_acc), grad_query)

    zero_pair = jnp.zeros((2, ext_rows, ext_cols, chan_width), jnp.float32)
    zero_table = jnp.zeros(
        (head_count, offset_rows + 2 * low_pad, lon_cols * ext_cols), jnp.float32
    )
    (grad_pair, table_acc), query_blocks = lax.scan(
        block_step, (zero_pair, zero_table), jnp.arange(block_count, dtype=jnp.int32)
    )
    grad_queries = query_blocks.reshape(lat_rows, lon_cols, chan_width)
    table_core = table_acc[:, low_pad : low_pad + offset_rows].reshape(
        head_count, offset_rows, lon_cols, ext_cols
    )
    col_take = (
        jnp.arange(lon_cols, dtype=jnp.int32)[:, None] + jnp.arange(WIN, dtype=jnp.int32)[None, :]
    )
    col_take = jnp.broadcast_to(
        col_take[None, None, :, :], (head_count, offset_rows, lon_cols, WIN)
    )
    table_local = jnp.sum(jnp.take_along_axis(table_core, col_take, axis=3), axis=2)
    grad_table = lax.psum(table_local, ("lat", "lon"))
    folded = fold_lat(fold_lon(grad_pair, lon_cols), lat_rows)
    grad_keys = folded[0].astype(jnp.bfloat16)
    grad_values = folded[1].astype(jnp.bfloat16)
    saved_out = attn_out.reshape(tokens, chan_width)
    slab_part = grad_cols
    grad_wout = lax.psum_scatter(
        jnp.dot(slab_part, saved_out, preferred_element_type=jnp.float32),
        ("lat", "lon"),
        scatter_dimension=0,
        tiled=True,
    )
    return (grad_queries, grad_keys, grad_values, grad_wout, grad_table)


def solution(mesh):
    return jax.shard_map(
        local,
        mesh=mesh,
        in_specs=(
            P("lat", "lon", "chan"),
            P("lat", "lon", "chan"),
            P("lat", "lon", "chan"),
            P("lat", "lon", "chan"),
            P("lat", "lon", "chan"),
            P(("lat", "lon"), "chan"),
            P("chan", None, None),
            P(),
        ),
        out_specs=(
            P("lat", "lon", "chan"),
            P("lat", "lon", "chan"),
            P("lat", "lon", "chan"),
            P(("lat", "lon"), "chan"),
            P("chan", None, None),
        ),
        check_vma=False,
    )
```

profile of v0, /device:TPU:240, one launch (start us, length us, event | category | flops | bytes accessed | tf_op | source)
XLA Modules:
  0.0 933.4 jit_solution(14924076082434811027)
XLA Ops:
  7.2 1.8 copy.63
  9.8 26.9 %all-gather.3.cloned.1.call-done = bf16[16,8,5120]{2,0,1:T(8,128)(2,1)} async-done(((bf16[16,8,1280]{2,0,1:T(8,128)(2,1)}), bf16[16,8,5120]{2,0,1:T(8,128)(2,1)}) %all-gather.3.cloned.1.call-update) | async-done | bytes 1310736 | tf_op jit(solution)/shard_map/all_gather | solution.py:79
  36.7 7.9 convolution_bitcast_fusion.1
  45.8 1.7 collective-permute-start.1
  51.5 4.6 collective-permute-start.3
  56.1 1.4 gather_fusion.1
  59.1 11.4 %collective-permute-done.3 = bf16[2,28,6,640]{3,0,2,1:T(2,128)(2,1)S(1)} collective-permute-done((bf16[2,28,6,640]{3,0,2,1:T(2,128)(2,1)S(1)}, bf16[2,28,6,640]{3,0,2,1:T(2,128)(2,1)S(1)}, u32[]{:S(2)}, u32[]{:S(2)}) %collective-permute-start.3) | collective-permute-done | bytes 430112 | tf_op jit(solution)/shard_map/ppermute | solution.py:18
  70.6 10.3 %collective-permute-done.2 = bf16[2,28,6,640]{3,0,2,1:T(2,128)(2,1)S(1)} collective-permute-done((bf16[2,28,6,640]{3,0,2,1:T(2,128)(2,1)S(1)}, bf16[2,28,6,640]{3,0,2,1:T(2,128)(2,1)S(1)}, u32[]{:S(2)}, u32[]{:S(2)}) %collective-permute-start.2) | collective-permute-done | bytes 430112 | tf_op jit(solution)/shard_map/ppermute | solution.py:17
  80.9 2.1 pad_maximum_fusion.1
  83.0 156.4 %all-gather.5.cloned.1.call-done = bf16[5120,640]{1,0:T(8,128)(2,1)} async-done(((bf16[80,640]{1,0:T(8,128)(2,1)}), bf16[5120,640]{1,0:T(8,128)(2,1)}) %all-gather.5.cloned.1.call-update) | async-done | bytes 6553616 | tf_op jit(solution)/shard_map/all_gather | solution.py:84
  239.4 4.6 fusion.42
  244.0 1.9 broadcast_in_dim.94
  245.9 117.0 %while.18 = (s32[]{:T(128)}, f32[2,28,20,640]{3,2,1,0:T(8,128)}, f32[5,31,160]{2,1,0:T(8,128)S(1)}, bf16[4,32,5,128]{3,1,2,0:T(8,128)(2,1)}, s32[4]{0:T(128)S(1)...) while((s32[]{:T(128)}, f32[2,28,20,640]{3,2,1,0:T(8,128)}, ...), condition=%wide.region_4.5_spmd.clone, body=%wide.region_0.0_spmd.clone.sunk | while | flops 67648624 | bytes 32509632 | solution.py:184
  257.6 1.3 constant_dynamic-slice_fusion.7
  259.8 1.9 dynamic-slice_bitcast_fusion.5
  272.1 3.0 fusion.106
  286.8 1.3 constant_dynamic-slice_fusion.7
  289.0 1.9 dynamic-slice_bitcast_fusion.5
  301.4 3.0 fusion.106
  316.0 1.3 constant_dynamic-slice_fusion.7
  318.3 1.9 dynamic-slice_bitcast_fusion.5
  330.6 3.1 fusion.106
  345.3 1.3 constant_dynamic-slice_fusion.7
  347.5 1.9 dynamic-slice_bitcast_fusion.5
  359.8 3.1 fusion.106
  363.0 2.2 convert.16
  367.6 2.0 collective-permute-start.4
  371.3 155.3 %gather_fusion.2 = f32[13000]{0:T(1024)S(1)} fusion(f32[5,25,8,20]{3,2,1,0:T(8,128)S(1)} %reshape.333, s32[13000]{0:T(1024)S(1)} %reshape.350), kind=kCustom, calls=%fused_computation.2 | custom fusion | bytes 312000 | tf_op jit(solution)/shard_map/jit(take_along_axis)/gather | solution.py:197
  529.9 2.3 fusion.59
  532.3 2.1 collective-permute-start.6
  534.3 4.4 collective-permute-start.7
  539.0 386.1 %psum.7 = f32[5,25,13]{2,1,0:T(8,128)S(1)} all-reduce(f32[5,25,13]{2,1,0:T(8,128)S(1)} %select_reduce_fusion), channel_id=1, replica_groups=mesh['lat'=8,'lon'=8,'chan'=4] {'lat','lon'}, use_global_device_ids=true, to_apply=%region_7.8 | all-reduce | flops 1625 | bytes 13000 | tf_op jit(solution)/shard_map/psum | solution.py:198
  (297 shorter events, 75.2 us)
Async XLA Ops:
  7.2 29.5 %copy-start = (bf16[16,8,640]{2,1,0:T(8,128)(2,1)S(1)}, bf16[16,8,640]{2,1,0:T(8,128)(2,1)}, u32[]{:S(2)}) copy-start(bf16[16,8,640]{2,1,0:T(8,128)(2,1)} %param.13) | copy-start | bytes 491524
  7.2 29.5 %all-gather.3.cloned.1.call-start = ((), (), s32[]{:S(2)}) async-start(), calls=%async_computation.1 | async-start | bytes 1638400 | tf_op jit(solution)/shard_map/all_gather | solution.py:79
  9.0 230.4 %all-gather.5.cloned.1.call-start = ((), (), s32[]{:S(2)}) async-start(), calls=%async_computation.2 | async-start | bytes 6656000 | tf_op jit(solution)/shard_map/all_gather | solution.py:84
  9.8 917.1 %reduce-scatter.2.cloned.1.call-start = ((), (), s32[]{:S(2)}) async-start(), calls=%async_computation.3 | async-start | bytes 13312000 | tf_op jit(solution)/shard_map/reduce_scatter | solution.py:204
  44.6 3.0 copy-start.8
  45.7 4.4 collective-permute-start
  45.8 4.8 collective-permute-start.1
  50.6 5.5 copy-start.1
  51.5 19.0 %collective-permute-start.3 = (bf16[2,28,6,640]{3,0,2,1:T(2,128)(2,1)S(1)}, bf16[2,28,6,640]{3,0,2,1:T(2,128)(2,1)S(1)}, u32[]{:S(2)}, u32[]{:S(2)}) collective-permute-start(bf16[2,28,6,640]{3,0,2,1:T(2,128)(2,1)S(1)} %copy.59), channel_id=1, source_target_pairs={{4,0},{8,4},{12,8},{16,12},{20,16},{24,20},{28,24},{0,28},{5,1},{9... | collective-permute-start | bytes 1290248 | tf_op jit(solution)/shard_map/ppermute | solution.py:18
  56.1 24.7 %collective-permute-start.2 = (bf16[2,28,6,640]{3,0,2,1:T(2,128)(2,1)S(1)}, bf16[2,28,6,640]{3,0,2,1:T(2,128)(2,1)S(1)}, u32[]{:S(2)}, u32[]{:S(2)}) collective-permute-start(bf16[2,28,6,640]{3,0,2,1:T(2,128)(2,1)S(1)} %copy.58), channel_id=1, source_target_pairs={{0,4},{4,8},{8,12},{12,16},{16,20},{20,24},{24,28},{28,0},{1,5},{5... | collective-permute-start | bytes 1290248 | tf_op jit(solution)/shard_map/ppermute | solution.py:17
  80.9 158.5 %copy-start.11 = (bf16[16,8,5120]{2,0,1:T(8,128)(2,1)S(1)}, bf16[16,8,5120]{2,0,1:T(8,128)(2,1)}, u32[]{:S(2)}) copy-start(bf16[16,8,5120]{2,0,1:T(8,128)(2,1)} %all-gather.3.cloned.1.call-done) | copy-start | bytes 3932164
  245.9 13.4 %copy-start.12 = (bf16[16,8,5,128]{3,1,2,0:T(8,128)(2,1)}, bf16[16,8,5,128]{3,1,2,0:T(8,128)(2,1)S(1)}, u32[]{:S(2)}) copy-start(bf16[16,8,5,128]{3,1,2,0:T(8,128)(2,1)S(1)} %get-tuple-element.541) | copy-start | bytes 491524 | tf_op jit(solution)/shard_map/while
  272.1 3.0 copy-start.13
  275.2 13.4 %copy-start.12 = (bf16[16,8,5,128]{3,1,2,0:T(8,128)(2,1)}, bf16[16,8,5,128]{3,1,2,0:T(8,128)(2,1)S(1)}, u32[]{:S(2)}) copy-start(bf16[16,8,5,128]{3,1,2,0:T(8,128)(2,1)S(1)} %get-tuple-element.541) | copy-start | bytes 491524 | tf_op jit(solution)/shard_map/while
  301.4 3.0 copy-start.13
  304.4 13.4 %copy-start.12 = (bf16[16,8,5,128]{3,1,2,0:T(8,128)(2,1)}, bf16[16,8,5,128]{3,1,2,0:T(8,128)(2,1)S(1)}, u32[]{:S(2)}) copy-start(bf16[16,8,5,128]{3,1,2,0:T(8,128)(2,1)S(1)} %get-tuple-element.541) | copy-start | bytes 491524 | tf_op jit(solution)/shard_map/while
  330.6 3.1 copy-start.13
  333.6 13.4 %copy-start.12 = (bf16[16,8,5,128]{3,1,2,0:T(8,128)(2,1)}, bf16[16,8,5,128]{3,1,2,0:T(8,128)(2,1)S(1)}, u32[]{:S(2)}) copy-start(bf16[16,8,5,128]{3,1,2,0:T(8,128)(2,1)S(1)} %get-tuple-element.541) | copy-start | bytes 491524 | tf_op jit(solution)/shard_map/while
  359.8 3.1 copy-start.13
  365.3 4.3 copy-start.4
  365.3 4.3 copy-start.6
  365.3 4.7 copy-start.14
  367.6 159.4 %collective-permute-start.5 = (bf16[2,28,6,640]{3,0,2,1:T(2,128)(2,1)}, bf16[2,28,6,640]{3,0,2,1:T(2,128)(2,1)}, u32[]{:S(2)}, u32[]{:S(2)}) collective-permute-start(bf16[2,28,6,640]{3,0,2,1:T(2,128)(2,1)} %copy.71), channel_id=1, source_target_pairs={{4,0},{8,4},{12,8},{16,12},{20,16},{24,20},{28,24},{0,28},{5,1},{9... | collective-permute-start | bytes 1290248 | tf_op jit(solution)/shard_map/ppermute | solution.py:18
  367.6 160.5 %collective-permute-start.4 = (bf16[2,28,6,640]{3,0,2,1:T(2,128)(2,1)}, bf16[2,28,6,640]{3,0,2,1:T(2,128)(2,1)}, u32[]{:S(2)}, u32[]{:S(2)}) collective-permute-start(bf16[2,28,6,640]{3,0,2,1:T(2,128)(2,1)} %copy.70), channel_id=1, source_target_pairs={{0,4},{4,8},{8,12},{12,16},{16,20},{20,24},{24,28},{28,0},{1,5},{5... | collective-permute-start | bytes 1290248 | tf_op jit(solution)/shard_map/ppermute | solution.py:17
  526.6 2.6 copy-start.5
  526.6 2.6 copy-start.7
  529.9 8.9 copy-start.16
  529.9 8.9 copy-start.18
  529.9 8.9 copy-start.20
  532.2 393.8 %copy-start.22 = (pred[16]{0:T(512)(128)(4,1)S(1)}, pred[16]{0:T(512)(128)(4,1)}, u32[]{:S(2)}) copy-start(pred[16]{0:T(512)(128)(4,1)} %constant.227.clone.1) | copy-start | bytes 52
  532.3 393.6 %collective-permute-start.6 = (bf16[2,6,8,640]{3,2,1,0:T(8,128)(2,1)S(1)}, bf16[2,6,8,640]{3,2,1,0:T(8,128)(2,1)S(1)}, u32[]{:S(2)}, u32[]{:S(2)}) collective-permute-start(bf16[2,6,8,640]{3,2,1,0:T(8,128)(2,1)S(1)} %get-tuple-element.361), channel_id=1, source_target_pairs={{0,32},{32,64},{64,96},{96,128},{128,160},{160,192},{192,224},{1,3... | collective-permute-start | bytes 368648 | tf_op jit(solution)/shard_map/ppermute | solution.py:17
  534.3 391.5 %collective-permute-start.7 = (bf16[2,6,8,640]{3,2,1,0:T(8,128)(2,1)S(1)}, bf16[2,6,8,640]{3,2,1,0:T(8,128)(2,1)S(1)}, u32[]{:S(2)}, u32[]{:S(2)}) collective-permute-start(bf16[2,6,8,640]{3,2,1,0:T(8,128)(2,1)S(1)} %get-tuple-element.362), channel_id=1, source_target_pairs={{32,0},{64,32},{96,64},{128,96},{160,128},{192,160},{224,192},{33,... | collective-permute-start | bytes 368648 | tf_op jit(solution)/shard_map/ppermute | solution.py:18
  (14 other events, 18.8 us)
Sparse Core Ops, SparseCore 0:
  9.8 26.8 all-gather.2
  38.5 200.8 all-gather.4
  242.6 461.3 reduce-scatter.1
where the time goes:
time: 935 us; the launch traced here: 933 us
  blocking collectives  386 us (41%)
  local copies, waits for them, and re-layouts  227 us (24%)
  waiting for transfers between devices  207 us (22%)
  loops' own time  33.7 us (4%)
  other arithmetic  28.7 us (3%)
  matrix products  21.7 us (2%)
  starting transfers between devices  15.1 us (2%)
  between operations  14.2 us (2%)
    psum x1, blocking collectives, local(): grad_table = lax.psum(table_local, ('lat', 'lon'))  386 us
    all_gather x1, waiting for transfers between devices, local(): lax.all_gather(w_out, ('lat', 'lon'), axis=0, tiled=True)  156 us
    gather x3, local copies, waits for them, and re-layouts, local(): jnp.take_along_axis(table_core, col_take, axis=3)  156 us
    another operation x1, loops' own time, local(): lax.scan(block_step, (zero_pair, zero_table), jnp.arange(block_count, dty...  33.7 us
    all_gather x1, waiting for transfers between devices, local(): lax.all_gather(grad_out, 'chan', axis=2, tiled=True).reshape(tokens, -1)  26.9 us
  transfers between devices with their start and end apart: 11, of which 6 were waited for; matrix products, arithmetic and copies ran while one was open for 29% of the time, Pallas kernels for 0%

commit v1 on v0

--- a/solution.py
+++ b/solution.py
@@ -5,6 +5,12 @@
 
 HEAD_DIM = 128
 WIN = 13
+
+
+def leaf_register(message, which_axis, axis_key):
+    for dev_i in (which_axis, axis_key):
+        message = lax.psum(message, dev_i)
+    return message
 
 
 def extended_2(value, sides, width, wrap):
@@ -195,7 +201,7 @@
         col_take[None, None, :, :], (head_count, offset_rows, lon_cols, WIN)
     )
     table_local = jnp.sum(jnp.take_along_axis(table_core, col_take, axis=3), axis=2)
-    grad_table = lax.psum(table_local, ("lat", "lon"))
+    grad_table = leaf_register(table_local, "lat", "lon")
     folded = fold_lat(fold_lon(grad_pair, lon_cols), lat_rows)
     grad_keys = folded[0].astype(jnp.bfloat16)
     grad_values = folded[1].astype(jnp.bfloat16)

time: 935 us -> 720 us (0.77)
  blocking collectives: 386 us -> 91 us
  waiting for transfers between devices: 207 us -> 288 us
    psum x1 -> x2, blocking collectives: 386 us -> 91 us  [leaf_register(): message = lax.psum(message, dev_i)]
    reduce_scatter x1, waiting for transfers between devices: 0.01 us -> 79.7 us  [local(): lax.psum_scatter(jnp.dot(slab_part, saved_out, preferred_element_type=jnp...]
  transfers between devices with their start and end apart: 11 -> 11, of which waited for: 6 -> 7; matrix products, arithmetic and copies ran while one was open for 29% -> 38% of each run, Pallas kernels for 0% -> 0%
where the time goes in v1:
time: 720 us; the launch traced here: 718 us
  waiting for transfers between devices  288 us (40%)
  local copies, waits for them, and re-layouts  227 us (32%)
  blocking collectives  91 us (13%)
  loops' own time  33.9 us (5%)
  other arithmetic  28.8 us (4%)
  matrix products  21.7 us (3%)
  starting transfers between devices  14.2 us (2%)
  between operations  14.2 us (2%)
    all_gather x1, waiting for transfers between devices, local(): lax.all_gather(w_out, ('lat', 'lon'), axis=0, tiled=True)  157 us
    gather x3, local copies, waits for them, and re-layouts, local(): jnp.take_along_axis(table_core, col_take, axis=3)  156 us
    psum x2, blocking collectives, leaf_register(): message = lax.psum(message, dev_i)  91 us
    reduce_scatter x1, waiting for transfers between devices, local(): lax.psum_scatter(jnp.dot(slab_part, saved_out, preferred_element_type=jnp...  79.7 us
    another operation x1, loops' own time, local(): lax.scan(block_step, (zero_pair, zero_table), jnp.arange(block_count, dty...  33.9 us
    all_gather x1, waiting for transfers between devices, local(): lax.all_gather(grad_out, 'chan', axis=2, tiled=True).reshape(tokens, -1)  26.9 us
  transfers between devices with their start and end apart: 11, of which 7 were waited for; matrix products, arithmetic and copies ran while one was open for 38% of the time, Pallas kernels for 0%

profile of v1, /device:TPU:240, one launch (start us, length us, event | category | flops | bytes accessed | tf_op | source)
XLA Modules:
  0.0 718.4 jit_solution(3827037467602790548)
XLA Ops:
  7.2 1.8 copy.63
  9.8 26.9 %all-gather.3.cloned.1.call-done = bf16[16,8,5120]{2,0,1:T(8,128)(2,1)} async-done(((bf16[16,8,1280]{2,0,1:T(8,128)(2,1)}), bf16[16,8,5120]{2,0,1:T(8,128)(2,1)}) %all-gather.3.cloned.1.call-update) | async-done | bytes 1310736 | tf_op jit(solution)/shard_map/all_gather | solution.py:85
  36.7 7.9 %convolution_bitcast_fusion.1 = f32[5120,640]{1,0:T(8,128)} fusion(bf16[16,8,5120]{2,0,1:T(8,128)(2,1)} %all-gather.3.cloned.1.call-done, bf16[16,8,640]{2,1,0:T(8,128)(2,1)S(1)} %copy-done), kind=kOutput, calls=%fused_computation.77 | convolution fusion | flops 838860800 | bytes 14581760 | tf_op jit(solution)/shard_map/dot_general | solution.py:211
  45.8 1.7 collective-permute-start.1
  51.5 4.6 collective-permute-start.3
  56.2 1.4 gather_fusion.1
  59.1 11.3 %collective-permute-done.3 = bf16[2,28,6,640]{3,0,2,1:T(2,128)(2,1)S(1)} collective-permute-done((bf16[2,28,6,640]{3,0,2,1:T(2,128)(2,1)S(1)}, bf16[2,28,6,640]{3,0,2,1:T(2,128)(2,1)S(1)}, u32[]{:S(2)}, u32[]{:S(2)}) %collective-permute-start.3) | collective-permute-done | bytes 430112 | tf_op jit(solution)/shard_map/ppermute | solution.py:24
  70.5 10.5 %collective-permute-done.2 = bf16[2,28,6,640]{3,0,2,1:T(2,128)(2,1)S(1)} collective-permute-done((bf16[2,28,6,640]{3,0,2,1:T(2,128)(2,1)S(1)}, bf16[2,28,6,640]{3,0,2,1:T(2,128)(2,1)S(1)}, u32[]{:S(2)}, u32[]{:S(2)}) %collective-permute-start.2) | collective-permute-done | bytes 430112 | tf_op jit(solution)/shard_map/ppermute | solution.py:23
  81.0 2.1 pad_maximum_fusion.1
  83.1 157.3 %all-gather.5.cloned.1.call-done = bf16[5120,640]{1,0:T(8,128)(2,1)} async-done(((bf16[80,640]{1,0:T(8,128)(2,1)}), bf16[5120,640]{1,0:T(8,128)(2,1)}) %all-gather.5.cloned.1.call-update) | async-done | bytes 6553616 | tf_op jit(solution)/shard_map/all_gather | solution.py:90
  240.4 4.6 fusion.42
  245.0 1.9 broadcast_in_dim.94
  246.9 117.3 %while.18 = (s32[]{:T(128)}, f32[2,28,20,640]{3,2,1,0:T(8,128)}, f32[5,31,160]{2,1,0:T(8,128)S(1)}, bf16[4,32,5,128]{3,1,2,0:T(8,128)(2,1)}, s32[4]{0:T(128)S(1)...) while((s32[]{:T(128)}, f32[2,28,20,640]{3,2,1,0:T(8,128)}, ...), condition=%wide.region_4.5_spmd.clone, body=%wide.region_0.0_spmd.clone.sunk | while | flops 67648624 | bytes 32509632 | solution.py:190
  258.6 1.3 constant_dynamic-slice_fusion.7
  260.8 1.9 dynamic-slice_bitcast_fusion.5
  273.2 3.1 fusion.106
  290.1 1.9 dynamic-slice_bitcast_fusion.5
  302.5 3.1 fusion.106
  319.4 1.9 dynamic-slice_bitcast_fusion.5
  331.7 3.1 fusion.106
  346.5 1.3 constant_dynamic-slice_fusion.7
  348.7 1.9 dynamic-slice_bitcast_fusion.5
  361.1 3.1 fusion.106
  364.2 2.2 convert.16
  368.8 2.0 collective-permute-start.4
  372.5 155.3 %gather_fusion.2 = f32[13000]{0:T(1024)S(1)} fusion(f32[5,25,8,20]{3,2,1,0:T(8,128)S(1)} %reshape.333, s32[13000]{0:T(1024)S(1)} %reshape.350), kind=kCustom, calls=%fused_computation.2 | custom fusion | bytes 312000 | tf_op jit(solution)/shard_map/jit(take_along_axis)/gather | solution.py:203
  531.1 2.4 fusion.59
  533.5 1.9 collective-permute-start.6
  535.4 3.7 collective-permute-start.7
  539.3 34.0 %psum.14 = f32[5,25,13]{2,1,0:T(8,128)S(1)} all-reduce(f32[5,25,13]{2,1,0:T(8,128)S(1)} %select_reduce_fusion), channel_id=1, replica_groups=mesh['lat'=8,'lon'=8,'chan'=4] {'lat'}, use_global_device_ids=true, to_apply=%region_7.8 | all-reduce | flops 1625 | bytes 13000 | tf_op jit(solution)/shard_map/psum | solution.py:12
  573.3 57.0 %psum.15 = f32[5,25,13]{2,1,0:T(8,128)S(1)} all-reduce(f32[5,25,13]{2,1,0:T(8,128)S(1)} %psum.14), channel_id=1, replica_groups=mesh['lat'=8,'lon'=8,'chan'=4] {'lon'}, use_global_device_ids=true, to_apply=%region_8.9 | all-reduce | flops 1625 | bytes 13000 | tf_op jit(solution)/shard_map/psum | solution.py:12
  632.1 79.7 %reduce-scatter.2.cloned.1.call-done = f32[80,640]{1,0:T(8,128)} async-done(((f32[5120,640]{1,0:T(8,128)}), f32[80,640]{1,0:T(8,128)}) %reduce-scatter.2.cloned.1.call-update) | async-done | bytes 204816 | tf_op jit(solution)/shard_map/reduce_scatter | solution.py:210
  (298 shorter events, 77.7 us)
Async XLA Ops:
  7.2 29.5 %copy-start = (bf16[16,8,640]{2,1,0:T(8,128)(2,1)S(1)}, bf16[16,8,640]{2,1,0:T(8,128)(2,1)}, u32[]{:S(2)}) copy-start(bf16[16,8,640]{2,1,0:T(8,128)(2,1)} %param.13) | copy-start | bytes 491524
  7.2 29.5 %all-gather.3.cloned.1.call-start = ((), (), s32[]{:S(2)}) async-start(), calls=%async_computation.1 | async-start | bytes 1638400 | tf_op jit(solution)/shard_map/all_gather | solution.py:85
  9.0 231.4 %all-gather.5.cloned.1.call-start = ((), (), s32[]{:S(2)}) async-start(), calls=%async_computation.2 | async-start | bytes 6656000 | tf_op jit(solution)/shard_map/all_gather | solution.py:90
  9.8 702.0 %reduce-scatter.2.cloned.1.call-start = ((), (), s32[]{:S(2)}) async-start(), calls=%async_computation.3 | async-start | bytes 13312000 | tf_op jit(solution)/shard_map/reduce_scatter | solution.py:210
  44.7 3.0 copy-start.8
  45.7 4.4 collective-permute-start
  45.8 4.8 collective-permute-start.1
  50.6 5.5 copy-start.1
  51.5 18.9 %collective-permute-start.3 = (bf16[2,28,6,640]{3,0,2,1:T(2,128)(2,1)S(1)}, bf16[2,28,6,640]{3,0,2,1:T(2,128)(2,1)S(1)}, u32[]{:S(2)}, u32[]{:S(2)}) collective-permute-start(bf16[2,28,6,640]{3,0,2,1:T(2,128)(2,1)S(1)} %copy.59), channel_id=1, source_target_pairs={{4,0},{8,4},{12,8},{16,12},{20,16},{24,20},{28,24},{0,28},{5,1},{9... | collective-permute-start | bytes 1290248 | tf_op jit(solution)/shard_map/ppermute | solution.py:24
  56.1 24.8 %collective-permute-start.2 = (bf16[2,28,6,640]{3,0,2,1:T(2,128)(2,1)S(1)}, bf16[2,28,6,640]{3,0,2,1:T(2,128)(2,1)S(1)}, u32[]{:S(2)}, u32[]{:S(2)}) collective-permute-start(bf16[2,28,6,640]{3,0,2,1:T(2,128)(2,1)S(1)} %copy.58), channel_id=1, source_target_pairs={{0,4},{4,8},{8,12},{12,16},{16,20},{20,24},{24,28},{28,0},{1,5},{5... | collective-permute-start | bytes 1290248 | tf_op jit(solution)/shard_map/ppermute | solution.py:23
  81.0 159.4 %copy-start.11 = (bf16[16,8,5120]{2,0,1:T(8,128)(2,1)S(1)}, bf16[16,8,5120]{2,0,1:T(8,128)(2,1)}, u32[]{:S(2)}) copy-start(bf16[16,8,5120]{2,0,1:T(8,128)(2,1)} %all-gather.3.cloned.1.call-done) | copy-start | bytes 3932164
  246.9 13.4 %copy-start.12 = (bf16[16,8,5,128]{3,1,2,0:T(8,128)(2,1)}, bf16[16,8,5,128]{3,1,2,0:T(8,128)(2,1)S(1)}, u32[]{:S(2)}) copy-start(bf16[16,8,5,128]{3,1,2,0:T(8,128)(2,1)S(1)} %get-tuple-element.541) | copy-start | bytes 491524 | tf_op jit(solution)/shard_map/while
  273.2 3.1 copy-start.13
  276.2 13.4 %copy-start.12 = (bf16[16,8,5,128]{3,1,2,0:T(8,128)(2,1)}, bf16[16,8,5,128]{3,1,2,0:T(8,128)(2,1)S(1)}, u32[]{:S(2)}) copy-start(bf16[16,8,5,128]{3,1,2,0:T(8,128)(2,1)S(1)} %get-tuple-element.541) | copy-start | bytes 491524 | tf_op jit(solution)/shard_map/while
  302.4 3.1 copy-start.13
  305.5 13.4 %copy-start.12 = (bf16[16,8,5,128]{3,1,2,0:T(8,128)(2,1)}, bf16[16,8,5,128]{3,1,2,0:T(8,128)(2,1)S(1)}, u32[]{:S(2)}) copy-start(bf16[16,8,5,128]{3,1,2,0:T(8,128)(2,1)S(1)} %get-tuple-element.541) | copy-start | bytes 491524 | tf_op jit(solution)/shard_map/while
  331.7 3.1 copy-start.13
  334.8 13.4 %copy-start.12 = (bf16[16,8,5,128]{3,1,2,0:T(8,128)(2,1)}, bf16[16,8,5,128]{3,1,2,0:T(8,128)(2,1)S(1)}, u32[]{:S(2)}) copy-start(bf16[16,8,5,128]{3,1,2,0:T(8,128)(2,1)S(1)} %get-tuple-element.541) | copy-start | bytes 491524 | tf_op jit(solution)/shard_map/while
  361.1 3.1 copy-start.13
  366.5 4.3 copy-start.4
  366.5 4.3 copy-start.6
  366.5 4.7 copy-start.14
  368.8 159.4 %collective-permute-start.5 = (bf16[2,28,6,640]{3,0,2,1:T(2,128)(2,1)}, bf16[2,28,6,640]{3,0,2,1:T(2,128)(2,1)}, u32[]{:S(2)}, u32[]{:S(2)}) collective-permute-start(bf16[2,28,6,640]{3,0,2,1:T(2,128)(2,1)} %copy.71), channel_id=1, source_target_pairs={{4,0},{8,4},{12,8},{16,12},{20,16},{24,20},{28,24},{0,28},{5,1},{9... | collective-permute-start | bytes 1290248 | tf_op jit(solution)/shard_map/ppermute | solution.py:24
  368.8 160.5 %collective-permute-start.4 = (bf16[2,28,6,640]{3,0,2,1:T(2,128)(2,1)}, bf16[2,28,6,640]{3,0,2,1:T(2,128)(2,1)}, u32[]{:S(2)}, u32[]{:S(2)}) collective-permute-start(bf16[2,28,6,640]{3,0,2,1:T(2,128)(2,1)} %copy.70), channel_id=1, source_target_pairs={{0,4},{4,8},{8,12},{12,16},{16,20},{20,24},{24,28},{28,0},{1,5},{5... | collective-permute-start | bytes 1290248 | tf_op jit(solution)/shard_map/ppermute | solution.py:23
  527.8 2.6 copy-start.5
  527.8 2.6 copy-start.7
  531.1 8.0 %copy-start.16 = (s32[8,13]{1,0:T(8,128)S(1)}, s32[8,13]{1,0:T(8,128)}, u32[]{:S(2)}) copy-start(s32[8,13]{1,0:T(8,128)} %copy-done.15) | copy-start | bytes 1252
  531.1 8.0 %copy-start.18 = (s32[8,13]{1,0:T(8,128)S(1)}, s32[8,13]{1,0:T(8,128)}, u32[]{:S(2)}) copy-start(s32[8,13]{1,0:T(8,128)} %copy-done.17) | copy-start | bytes 1252
  531.1 8.1 %copy-start.20 = (pred[8,13]{1,0:T(8,128)(4,1)S(1)}, pred[8,13]{1,0:T(8,128)(4,1)}, u32[]{:S(2)}) copy-start(pred[8,13]{1,0:T(8,128)(4,1)} %copy-done.19) | copy-start | bytes 316
  533.5 97.7 %copy-start.22 = (pred[16]{0:T(512)(128)(4,1)S(1)}, pred[16]{0:T(512)(128)(4,1)}, u32[]{:S(2)}) copy-start(pred[16]{0:T(512)(128)(4,1)} %constant.227.clone.1) | copy-start | bytes 52
  533.5 97.6 %collective-permute-start.6 = (bf16[2,6,8,640]{3,2,1,0:T(8,128)(2,1)S(1)}, bf16[2,6,8,640]{3,2,1,0:T(8,128)(2,1)S(1)}, u32[]{:S(2)}, u32[]{:S(2)}) collective-permute-start(bf16[2,6,8,640]{3,2,1,0:T(8,128)(2,1)S(1)} %get-tuple-element.361), channel_id=1, source_target_pairs={{0,32},{32,64},{64,96},{96,128},{128,160},{160,192},{192,224},{1,3... | collective-permute-start | bytes 368648 | tf_op jit(solution)/shard_map/ppermute | solution.py:23
  535.4 95.7 %collective-permute-start.7 = (bf16[2,6,8,640]{3,2,1,0:T(8,128)(2,1)S(1)}, bf16[2,6,8,640]{3,2,1,0:T(8,128)(2,1)S(1)}, u32[]{:S(2)}, u32[]{:S(2)}) collective-permute-start(bf16[2,6,8,640]{3,2,1,0:T(8,128)(2,1)S(1)} %get-tuple-element.362), channel_id=1, source_target_pairs={{32,0},{64,32},{96,64},{128,96},{160,128},{192,160},{224,192},{33,... | collective-permute-start | bytes 368648 | tf_op jit(solution)/shard_map/ppermute | solution.py:24
  (14 other events, 18.8 us)
Sparse Core Ops, SparseCore 0:
  9.8 26.8 all-gather.2
  38.5 201.8 all-gather.4
  243.5 468.2 reduce-scatter.1
